TPU v7x, 32 devices: a whole 2x2x4 slice. The times are simulated.
32 devices in a mesh: lm: 8 (over z, x), kf: 4 (over y, core).
Axes of the slice: x: 2, y: 2, z: 4, core: 2. Of those that a mesh axis runs over, the one named last changes fastest.
Arguments:
- residual_rows: bfloat16 [4096, 128], P(('lm', 'kf')), may hold values from -6 to 6
- jacobian: bfloat16 [4096, 15, 128], P(('lm', 'kf')), may hold values from -1.5 to 1.5
- nullspace: bfloat16 [4096, 128, 128], P(('lm', 'kf')), may hold values from -0.5 to 0.5
- frame_ids: int32 [4096, 64], P(('lm', 'kf')), may hold values from 0 to 16383, as said below
- obs_count: int32 [4096], P(('lm', 'kf')), may hold values from 4 to 64
- damping: float32 [15, 16384], P(None, 'kf'), may hold values from 1 to 10
- jacobi_scale: float32 [15, 16384], P(None, 'kf'), may hold values from 0.02 to 0.3
Outputs:
- solution: float32 [15, 16384], P(None, 'kf')
- residual: float32 [15, 16384], P(None, 'kf')
Inputs may be any that keep to these rules, and one draw needn't show every extreme that they name: `frame_ids`: within a block the keyframe ids rise strictly from slot to slot by 1 to 8. A block stored on the device with kf index w names only keyframes from 4096 * w up to but not including 4096 * (w + 2), and never one of 16384 or more.
All inputs are finite; a program needn't handle non-finite values.
Results may differ from a plain program's by a relative error of at most 0.005.
Values sent between devices are 32-bit elements; how exact they have to be, the bound alone decides.
A program may use at most 64 MiB of HBM per device.

v0:
```python
import jax
import jax.numpy as jnp
from jax import lax
from jax.sharding import PartitionSpec as P

ITERS = 2


def passed_along(array, axis, by):
    length = lax.axis_size(axis)
    pairs = [(i, i + by) for i in range(length) if 0 <= i + by < length]
    return lax.ppermute(array, axis, pairs)


def row_layout(frame_ids, obs_count, first_frame):
    slots = lax.broadcasted_iota(jnp.int32, frame_ids.shape, 1)
    live = (slots < obs_count[:, None]).astype(jnp.float32)
    return (jnp.repeat(frame_ids - first_frame, 2, axis=1), jnp.repeat(live, 2, axis=1))


def project(lifted, nullspace, live):
    lifted_half = (lifted * live).astype(jnp.bfloat16)
    inner = jnp.einsum(
        "brk,br->bk", nullspace, lifted_half, preferred_element_type=jnp.float32
    ).astype(jnp.bfloat16)
    spread = jnp.einsum("brk,bk->br", nullspace, inner, preferred_element_type=jnp.float32)
    return spread * live


def spread_back(spread, jacobian, row_ids, width):
    terms = jacobian * spread[:, None, :]
    terms = jnp.moveaxis(terms, 1, 0).reshape(jacobian.shape[1], -1)
    return jnp.zeros((jacobian.shape[1], width), jnp.float32).at[:, row_ids.reshape(-1)].add(terms)


def window_pair(field):
    return jnp.concatenate([field, passed_along(field, "kf", -1)], axis=1)


def fold_next(partial_value, frames):
    return partial_value[:, :frames] + passed_along(partial_value[:, frames:], "kf", 1)


def inner_window(left, right):
    return lax.psum(jnp.sum(left * right), "kf")


def shards(residual_rows, jacobian, nullspace, frame_ids, obs_count, damping, jacobi_scale):
    frames = damping.shape[1]
    row_ids, live = row_layout(frame_ids, obs_count, lax.axis_index("kf") * frames)

    def local_terms(window_field):
        if window_field is None:
            lifted = residual_rows.astype(jnp.float32)
        else:
            gathered = jnp.take(window_field, row_ids, axis=1)
            lifted = jnp.sum(jacobian * jnp.moveaxis(gathered, 0, 1), axis=1)
        return spread_back(project(lifted, nullspace, live), jacobian, row_ids, 2 * frames)

    def combine(partial_value):
        return lax.psum(fold_next(partial_value, frames), "lm")

    damp_part, scale_part = (damping, jacobi_scale)
    gradient = -combine(local_terms(None))
    residual = gradient
    solution = jnp.zeros_like(gradient)
    scaled = scale_part * residual
    direction = scaled
    energy = inner_window(residual, scaled)
    for step_index in range(ITERS):
        applied = combine(local_terms(window_pair(direction))) + damp_part * direction
        step_size = energy / inner_window(direction, applied)
        solution = solution + step_size * direction
        residual = residual - step_size * applied
        if step_index + 1 < ITERS:
            scaled = scale_part * residual
            fresh = inner_window(residual, scaled)
            direction = scaled + fresh / energy * direction
            energy = fresh
    return (solution, residual)


def solution(mesh):
    placed = (
        P(("lm", "kf"), None),
        P(("lm", "kf"), None, None),
        P(("lm", "kf"), None, None),
        P(("lm", "kf"), None),
        P(("lm", "kf")),
        P(None, "kf"),
        P(None, "kf"),
    )
    return jax.shard_map(
        shards,
        mesh=mesh,
        in_specs=placed,
        out_specs=(P(None, "kf"), P(None, "kf")),
        check_vma=False,
    )
```

profile of v0, /device:TPU:0, one launch (start us, length us, event | category | flops | bytes accessed | tf_op | source)
XLA Modules:
  0.0 765.3 jit_solution(5595085198218443961)
XLA Ops:
  9.0 3.5 fusion.28
  15.1 4.3 broadcast_in_dim.13.clone
  19.4 5.5 reshape_reshape.2
  25.1 4.7 copy.161
  29.8 89.9 %scatter_custom_fusion = f32[15,8192]{0,1:T(8,128)} fusion(s32[16384]{0:T(1024)S(1)} %bitcast.77, f32[16384,15]{1,0:T(8,128)} %bitcast.65, f32[]{:T(128)} %constant.1.clone.1), kind=kCustom, calls=%fused_computation.9 | custom fusion | flops 245760 | bytes 492032 | tf_op jit(solution)/shard_map/scatter-add | solution.py:33
  119.6 3.8 fusion.27
  123.5 3.0 copy.130
  126.4 3.1 collective-permute-start
  132.5 77.6 %all-reduce.5.cloned.1.call-done = f32[15,4096]{1,0:T(8,128)} async-done(((f32[15,4096]{1,0:T(8,128)}), f32[15,4096]{1,0:T(8,128)}) %all-reduce.5.cloned.1.call-update) | async-done | bytes 245776 | tf_op jit(solution)/shard_map/psum | solution.py:61
  214.5 2.7 copy.133
  217.2 56.6 %gather_fusion = f32[16384,15]{1,0:T(8,128)} fusion(f32[15,8192]{0,1:T(8,128)} %copy.133, s32[16384]{0:T(1024)S(1)} %bitcast_clamp_fusion), kind=kCustom, calls=%fused_computation.clone | custom fusion | bytes 2031616 | tf_op jit(solution)/shard_map/jit(_take)/gather | solution.py:56
  273.8 5.3 copy.134
  279.3 3.5 fusion.17
  285.4 4.7 copy.162
  290.1 89.9 %scatter_custom_fusion.1 = f32[15,8192]{0,1:T(8,128)} fusion(s32[16384]{0:T(1024)S(1)} %bitcast.78, f32[16384,15]{1,0:T(8,128)} %bitcast.66, f32[]{:T(128)} %constant.1.clone.1), kind=kCustom, calls=%fused_computation.7 | custom fusion | flops 245760 | bytes 492032 | tf_op jit(solution)/shard_map/scatter-add | solution.py:33
  380.0 3.8 fusion.26
  383.8 3.0 copy.139
  386.8 6.7 collective-permute-start.2
  396.7 72.9 %all-reduce.7.cloned.1.call-done = f32[15,4096]{1,0:T(8,128)} async-done(((f32[15,4096]{1,0:T(8,128)}), f32[15,4096]{1,0:T(8,128)}) %all-reduce.7.cloned.1.call-update) | async-done | bytes 245776 | tf_op jit(solution)/shard_map/psum | solution.py:61
  471.2 6.3 all-reduce
  481.3 7.2 psum.53
  493.3 2.7 copy.142
  496.0 56.6 %gather_fusion.1 = f32[16384,15]{1,0:T(8,128)} fusion(f32[15,8192]{0,1:T(8,128)} %copy.142, s32[16384]{0:T(1024)S(1)} %bitcast_clamp_fusion), kind=kCustom, calls=%fused_computation.1.clone | custom fusion | bytes 2031616 | tf_op jit(solution)/shard_map/jit(_take)/gather | solution.py:56
  552.6 5.4 copy.143
  558.1 3.5 fusion.13
  564.3 4.7 copy.163
  569.0 89.9 %scatter_custom_fusion.2 = f32[15,8192]{0,1:T(8,128)} fusion(s32[16384]{0:T(1024)} %bitcast.79, f32[16384,15]{1,0:T(8,128)} %bitcast.64, f32[]{:T(128)} %constant.1.clone.1), kind=kCustom, calls=%fused_computation.5 | custom fusion | flops 245760 | bytes 492032 | tf_op jit(solution)/shard_map/scatter-add | solution.py:33
  658.8 3.8 fusion.25
  662.7 3.0 copy.148
  665.6 6.1 collective-permute-start.4
  674.9 72.9 %all-reduce.9.cloned.1.call-done = f32[15,4096]{1,0:T(8,128)} async-done(((f32[15,4096]{1,0:T(8,128)}), f32[15,4096]{1,0:T(8,128)}) %all-reduce.9.cloned.1.call-update) | async-done | bytes 245776 | tf_op jit(solution)/shard_map/psum | solution.py:61
  749.4 6.3 psum.55
  (88 shorter events, 34.6 us)
Async XLA Ops:
  7.2 202.9 %all-reduce.5.cloned.1.call-start = ((), (), s32[]{:S(2)}) async-start(), calls=%async_computation | async-start | bytes 524288 | tf_op jit(solution)/shard_map/psum | solution.py:61
  8.9 3.6 copy-start
  8.9 6.0 copy-start.11
  15.1 9.9 %copy-start.3 = (bf16[128,15,128]{2,0,1:T(8,128)(2,1)S(1)}, bf16[128,15,128]{2,0,1:T(8,128)(2,1)}, u32[]{:S(2)}) copy-start(bf16[128,15,128]{2,0,1:T(8,128)(2,1)} %param.10) | copy-start | bytes 1474564
  25.0 265.1 %copy-start.10 = (s32[16384,1]{0,1:T(1,128)}, s32[16384,1]{0,1:T(1,128)S(1)}, u32[]{:S(2)}) copy-start(s32[16384,1]{0,1:T(1,128)S(1)} %compare_select_fusion) | copy-start | bytes 196612
  123.5 86.6 %copy-start.6 = (f32[15,4096]{1,0:T(8,128)S(1)}, f32[15,4096]{1,0:T(8,128)}, u32[]{:S(2)}) copy-start(f32[15,4096]{1,0:T(8,128)} %param.15) | copy-start | bytes 737284
  126.4 3.9 collective-permute-start
  132.0 337.5 %all-reduce.7.cloned.1.call-start = ((), (), s32[]{:S(2)}) async-start(), calls=%async_computation.1 | async-start | bytes 524288 | tf_op jit(solution)/shard_map/psum | solution.py:61
  132.2 147.0 %copy-start.8 = (f32[128,128]{1,0:T(8,128)}, f32[128,128]{1,0:T(8,128)S(1)}, u32[]{:S(2)}) copy-start(f32[128,128]{1,0:T(8,128)S(1)} %copy.135) | copy-start | bytes 196612
  211.0 3.4 collective-permute-start.1
  279.1 3.7 copy-start.1
  383.8 85.7 %copy-start.4 = (f32[15,4096]{1,0:T(8,128)S(1)}, f32[15,4096]{1,0:T(8,128)}, u32[]{:S(2)}) copy-start(f32[15,4096]{1,0:T(8,128)} %param.14) | copy-start | bytes 737284
  383.8 85.7 %copy-start.5 = (f32[15,4096]{1,0:T(8,128)S(1)}, f32[15,4096]{1,0:T(8,128)}, u32[]{:S(2)}) copy-start(f32[15,4096]{1,0:T(8,128)} %all-reduce.5.cloned.1.call-done) | copy-start | bytes 737284
  386.8 8.0 %collective-permute-start.2 = (f32[15,4096]{1,0:T(8,128)}, f32[15,4096]{1,0:T(8,128)}, u32[]{:S(2)}, u32[]{:S(2)}) collective-permute-start(f32[15,4096]{1,0:T(8,128)} %copy.139), channel_id=1, source_target_pairs={{0,1},{1,2},{2,3},{4,5},{5,6},{6,7},{8,9},{9,10},{10,11},{12,13},{... | collective-permute-start | bytes 737288 | tf_op jit(solution)/shard_map/ppermute | solution.py:12
  396.6 351.2 %all-reduce.9.cloned.1.call-start = ((), (), s32[]{:S(2)}) async-start(), calls=%async_computation.2 | async-start | bytes 524288 | tf_op jit(solution)/shard_map/psum | solution.py:61
  489.8 3.4 collective-permute-start.3
  552.6 5.5 copy-start.9
  557.9 3.7 copy-start.2
  662.7 94.3 %copy-start.7 = (f32[15,4096]{1,0:T(8,128)S(1)}, f32[15,4096]{1,0:T(8,128)}, u32[]{:S(2)}) copy-start(f32[15,4096]{1,0:T(8,128)} %get-tuple-element.19) | copy-start | bytes 737284
  665.6 7.5 collective-permute-start.4
Sparse Core Ops, SparseCore 0:
  132.2 77.8 all-reduce.4
  396.7 72.7 all-reduce.6
  675.0 72.7 all-reduce.8
where the time goes:
time: 766 us; the launch traced here: 765 us
  other arithmetic  285 us (37%)
  waiting for transfers between devices  227 us (30%)
  local copies, waits for them, and re-layouts  179 us (23%)
  blocking collectives  19.8 us (3%)
  starting transfers between devices  19 us (2%)
  between operations  18.1 us (2%)
  matrix products  17.3 us (2%)
    scatter-add x3, other arithmetic, spread_back(): jnp.zeros((jacobian.shape[1], width), jnp.float32)  270 us
    psum x3, waiting for transfers between devices, combine(): return lax.psum(fold_next(partial_value, frames), 'lm')  223 us
    gather x4, local copies, waits for them, and re-layouts, local_terms(): gathered = jnp.take(window_field, row_ids, axis=1)  124 us
    slice x6, local copies, waits for them, and re-layouts, fold_next(): partial_value[:, frames:]  20.4 us
    psum x3, blocking collectives, inner_window(): return lax.psum(jnp.sum(left * right), 'kf')  19.8 us
    ppermute x5, starting transfers between devices, passed_along(): return lax.ppermute(array, axis, pairs)  18.9 us
  transfers between devices with their start and end apart: 8, of which 6 were waited for; matrix products, arithmetic and copies ran while one was open for 0% of the time, Pallas kernels for 0%

commit v1 on v0

--- a/solution.py
+++ b/solution.py
@@ -58,7 +58,7 @@
         return spread_back(project(lifted, nullspace, live), jacobian, row_ids, 2 * frames)
 
     def combine(partial_value):
-        return lax.psum(fold_next(partial_value, frames), "lm")
+        return jnp.sum(lax.all_gather(fold_next(partial_value, frames), "lm"), axis=0)
 
     damp_part, scale_part = (damping, jacobi_scale)
     gradient = -combine(local_terms(None))

time: 766 us -> 702 us (0.916)
  waiting for transfers between devices: 227 us -> 164 us
    psum x3 -> x0, waiting for transfers between devices: 223 us -> none  [combine(): return lax.psum(fold_next(partial_value, frames), 'lm')]
    all_gather x0 -> x3, waiting for transfers between devices: none -> 157 us  [combine(): lax.all_gather(fold_next(partial_value, frames), 'lm')]
    slice x6 -> x9, local copies, waits for them, and re-layouts: 20.4 us -> 6.63 us  [fold_next(): partial_value[:, frames:]]
    unnamed x0 -> x3, other arithmetic: none -> 9.51 us
  transfers between devices with their start and end apart: 8 -> 8, of which waited for: 6 -> 8; matrix products, arithmetic and copies ran while one was open for 0% -> 0% of each run, Pallas kernels for 0% -> 0%
where the time goes in v1:
time: 702 us; the launch traced here: 701 us
  other arithmetic  289 us (41%)
  local copies, waits for them, and re-layouts  174 us (25%)
  waiting for transfers between devices  164 us (23%)
  blocking collectives  19.8 us (3%)
  starting transfers between devices  18.4 us (3%)
  between operations  18.3 us (3%)
  matrix products  17.3 us (2%)
    scatter-add x3, other arithmetic, spread_back(): jnp.zeros((jacobian.shape[1], width), jnp.float32)  270 us
    all_gather x3, waiting for transfers between devices, combine(): lax.all_gather(fold_next(partial_value, frames), 'lm')  157 us
    gather x4, local copies, waits for them, and re-layouts, local_terms(): gathered = jnp.take(window_field, row_ids, axis=1)  124 us
    psum x3, blocking collectives, inner_window(): return lax.psum(jnp.sum(left * right), 'kf')  19.8 us
    ppermute x5, starting transfers between devices, passed_along(): return lax.ppermute(array, axis, pairs)  18.3 us
    reshape x3, local copies, waits for them, and re-layouts, spread_back(): terms = jnp.moveaxis(terms, 1, 0).reshape(jacobian.shape[1], -1)  14.1 us
  transfers between devices with their start and end apart: 8, of which 8 were waited for; matrix products, arithmetic and copies ran while one was open for 0% of the time, Pallas kernels for 0%

profile of v1, /device:TPU:0, one launch (start us, length us, event | category | flops | bytes accessed | tf_op | source)
XLA Modules:
  0.0 701.4 jit_solution(12129009553198834177)
XLA Ops:
  9.0 3.5 fusion.28
  15.1 4.3 broadcast_in_dim.13.clone
  19.4 5.5 reshape_reshape.2
  25.1 4.7 copy.98
  29.8 89.9 %scatter_custom_fusion = f32[15,8192]{0,1:T(8,128)} fusion(s32[16384]{0:T(1024)S(1)} %bitcast.83, f32[16384,15]{1,0:T(8,128)} %bitcast.71, f32[]{:T(128)} %constant.1.clone.1), kind=kCustom, calls=%fused_computation.15 | custom fusion | flops 245760 | bytes 492032 | tf_op jit(solution)/shard_map/scatter-add | solution.py:33
  121.9 2.4 collective-permute-start
  126.1 3.2 fusion.2
  129.2 3.0 copy.65
  132.7 55.7 %all-gather.10.cloned.1.call-done = f32[8,15,4096]{2,1,0:T(8,128)} async-done(((f32[1,15,4096]{2,1,0:T(8,128)}), f32[8,15,4096]{2,1,0:T(8,128)}) %all-gather.10.cloned.1.call-update) | async-done | bytes 1966096 | tf_op jit(solution)/shard_map/all_gather | solution.py:61
  193.6 2.7 copy.68
  196.2 56.6 %gather_fusion = f32[16384,15]{1,0:T(8,128)} fusion(f32[15,8192]{0,1:T(8,128)} %copy.68, s32[16384]{0:T(1024)S(1)} %bitcast_clamp_fusion), kind=kCustom, calls=%fused_computation.clone | custom fusion | bytes 2031616 | tf_op jit(solution)/shard_map/jit(_take)/gather | solution.py:56
  252.8 5.3 copy.69
  258.4 3.5 fusion.20
  264.5 4.7 copy.99
  269.2 89.9 %scatter_custom_fusion.1 = f32[15,8192]{0,1:T(8,128)} fusion(s32[16384]{0:T(1024)} %bitcast.84, f32[16384,15]{1,0:T(8,128)} %bitcast.72, f32[]{:T(128)} %constant.1.clone.1), kind=kCustom, calls=%fused_computation.13 | custom fusion | flops 245760 | bytes 492032 | tf_op jit(solution)/shard_map/scatter-add | solution.py:33
  361.3 6.7 collective-permute-start.2
  370.1 3.2 fusion.1
  373.3 3.0 copy.75
  376.4 50.8 %all-gather.12.cloned.1.call-done = f32[8,15,4096]{2,1,0:T(8,128)} async-done(((f32[1,15,4096]{2,1,0:T(8,128)}), f32[8,15,4096]{2,1,0:T(8,128)}) %all-gather.12.cloned.1.call-update) | async-done | bytes 1966096 | tf_op jit(solution)/shard_map/all_gather | solution.py:61
  429.6 6.3 all-reduce
  438.7 7.2 %psum.30 = f32[]{:T(128)} all-reduce(f32[]{:T(128)} %get-tuple-element.13), channel_id=1, replica_groups=mesh['lm'=8,'kf'=4] {'kf'}, use_global_device_ids=true, to_apply=%region_10.12 | all-reduce | flops 1 | bytes 8 | tf_op jit(solution)/shard_map/psum | solution.py:45
  450.8 2.7 copy.78
  453.5 56.6 %gather_fusion.1 = f32[16384,15]{1,0:T(8,128)} fusion(f32[15,8192]{0,1:T(8,128)} %copy.78, s32[16384]{0:T(1024)S(1)} %bitcast_clamp_fusion), kind=kCustom, calls=%fused_computation.1.clone | custom fusion | bytes 2031616 | tf_op jit(solution)/shard_map/jit(_take)/gather | solution.py:56
  510.1 5.4 copy.79
  515.6 3.5 fusion.16
  521.8 4.7 copy.100
  526.4 89.9 %scatter_custom_fusion.2 = f32[15,8192]{0,1:T(8,128)} fusion(s32[16384]{0:T(1024)} %bitcast.85, f32[16384,15]{1,0:T(8,128)} %bitcast.70, f32[]{:T(128)} %constant.1.clone.1), kind=kCustom, calls=%fused_computation.11 | custom fusion | flops 245760 | bytes 492032 | tf_op jit(solution)/shard_map/scatter-add | solution.py:33
  618.5 6.1 collective-permute-start.4
  626.8 3.2 fusion
  630.0 3.0 copy.85
  633.0 51.0 %all-gather.14.cloned.1.call-done = f32[8,15,4096]{2,1,0:T(8,128)} async-done(((f32[1,15,4096]{2,1,0:T(8,128)}), f32[8,15,4096]{2,1,0:T(8,128)}) %all-gather.14.cloned.1.call-update) | async-done | bytes 1966096 | tf_op jit(solution)/shard_map/all_gather | solution.py:61
  686.4 6.3 psum.31
  (97 shorter events, 38.9 us)
Async XLA Ops:
  7.2 181.1 %all-gather.10.cloned.1.call-start = ((), (), s32[]{:S(2)}) async-start(), calls=%async_computation | async-start | bytes 2359296 | tf_op jit(solution)/shard_map/all_gather | solution.py:61
  8.9 3.6 copy-start
  8.9 6.0 copy-start.11
  15.1 9.9 %copy-start.3 = (bf16[128,15,128]{2,0,1:T(8,128)(2,1)S(1)}, bf16[128,15,128]{2,0,1:T(8,128)(2,1)}, u32[]{:S(2)}) copy-start(bf16[128,15,128]{2,0,1:T(8,128)(2,1)} %param.10) | copy-start | bytes 1474564
  25.0 4.8 copy-start.10
  119.7 1.6 slice-start.1
  121.9 3.5 collective-permute-start
  129.2 60.8 %copy-start.5 = (f32[15,4096]{1,0:T(8,128)S(1)}, f32[15,4096]{1,0:T(8,128)}, u32[]{:S(2)}) copy-start(f32[15,4096]{1,0:T(8,128)} %param.15) | copy-start | bytes 737284
  132.2 294.9 %all-gather.12.cloned.1.call-start = ((), (), s32[]{:S(2)}) async-start(), calls=%async_computation.1 | async-start | bytes 2359296 | tf_op jit(solution)/shard_map/all_gather | solution.py:61
  132.3 126.0 %copy-start.8 = (f32[128,128]{1,0:T(8,128)}, f32[128,128]{1,0:T(8,128)S(1)}, u32[]{:S(2)}) copy-start(f32[128,128]{1,0:T(8,128)S(1)} %copy.70) | copy-start | bytes 196612
  190.1 3.4 collective-permute-start.1
  258.2 3.7 copy-start.1
  359.0 1.6 slice-start.2
  361.3 7.3 %collective-permute-start.2 = (f32[15,4096]{1,0:T(8,128)S(1)}, f32[15,4096]{1,0:T(8,128)}, u32[]{:S(2)}, u32[]{:S(2)}) collective-permute-start(f32[15,4096]{1,0:T(8,128)S(1)} %copy.73), channel_id=1, source_target_pairs={{0,1},{1,2},{2,3},{4,5},{5,6},{6,7},{8,9},{9,10},{10,11},{12,13},{... | collective-permute-start | bytes 737288 | tf_op jit(solution)/shard_map/ppermute | solution.py:12
  370.1 58.7 %copy-start.4 = (f32[15,4096]{1,0:T(8,128)S(1)}, f32[15,4096]{1,0:T(8,128)}, u32[]{:S(2)}) copy-start(f32[15,4096]{1,0:T(8,128)} %param.14) | copy-start | bytes 737284
  373.3 64.0 %copy-start.6 = (f32[15,4096]{1,0:T(8,128)S(1)}, f32[15,4096]{1,0:T(8,128)}, u32[]{:S(2)}) copy-start(f32[15,4096]{1,0:T(8,128)} %param.15) | copy-start | bytes 737284
  376.3 307.7 %all-gather.14.cloned.1.call-start = ((), (), s32[]{:S(2)}) async-start(), calls=%async_computation.2 | async-start | bytes 2359296 | tf_op jit(solution)/shard_map/all_gather | solution.py:61
  447.3 3.4 collective-permute-start.3
  510.1 5.5 copy-start.9
  515.4 3.7 copy-start.2
  616.3 1.6 slice-start
  618.5 6.7 collective-permute-start.4
  630.0 64.0 %copy-start.7 = (f32[15,4096]{1,0:T(8,128)S(1)}, f32[15,4096]{1,0:T(8,128)}, u32[]{:S(2)}) copy-start(f32[15,4096]{1,0:T(8,128)} %get-tuple-element.15) | copy-start | bytes 737284
Sparse Core Ops, SparseCore 0:
  132.3 55.9 all-gather.9
  376.4 50.6 all-gather.11
  633.1 50.8 all-gather.13
